TPU v7x, 32 devices: a whole 2x2x4 slice. The times are simulated.
32 devices in a mesh: section: 4 (over y, core), expert: 8 (over z, x).
Axes of the slice: x: 2, y: 2, z: 4, core: 2. Of those that a mesh axis runs over, the one named last changes fastest.
Arguments:
- acts: bfloat16 [4, 512, 2048], P('section', 'expert'), may hold values from -6 to 6
- norm_gains: float32 [4, 2, 2048], P('section'), may hold values from 0.5 to 5.5
- w_query: bfloat16 [4, 2048, 1024], P('section', None, 'expert'), may hold values from -0.125 to 0.125
- w_keyval: bfloat16 [4, 2048, 4, 256], P('section', 'expert'), may hold values from -0.125 to 0.125
- w_out: bfloat16 [4, 1024, 2048], P('section', 'expert'), may hold values from -0.5 to 0.5
- w_gate_up: bfloat16 [4, 32, 2048, 1536], P('section', 'expert'), may hold values from -0.125 to 0.125
- w_down: bfloat16 [4, 32, 768, 2048], P('section', 'expert'), may hold values from -0.21875 to 0.21875
- expert_ids: int32 [4, 512, 8], P('section', 'expert'), may hold values from 0 to 31, all different within a row; in each aligned block of 64 rows (0 to 63, 64 to 127, ..., all dimensions but the last counted through in order) at most 24 rows name the same one
- gate_weights: float32 [4, 512, 8], P('section', 'expert'), may hold values from 0.05 to 0.3
- segment_ids: int32 [4, 512], P('section'), may hold values from 0 to 15, never falling along the last dimension, each value on 1 to 128 neighbouring positions
Outputs:
- handed: bfloat16 [4, 512, 2048], P('section', 'expert')
Inputs may be any that keep to these rules, and one draw needn't show every extreme that they name: `expert_ids`: A token names 8 different experts. In each section the tokens of one index of expert (aligned blocks of 64 tokens) name no expert more than 24 times, a bound that some block reaches. `segment_ids`: never falling along a section's positions; a segment holds at most 128 positions, and one exactly that many.
All inputs are finite; a program needn't handle non-finite values.
Results may differ from a plain program's by a relative error of at most 0.015.
The roundings to bfloat16 on the way count: a program that leaves them out, or rounds other values in their place, can miss the bound.
Values may be sent and summed in bfloat16 or wider, within the bound.
A program may use at most 128 MiB of HBM per device.

v0:
```python
import math
import jax
import jax.numpy as jnp
from jax import lax
from jax.sharding import PartitionSpec as P

HD = 128
KV = 4
EXPERTS = 32
TOPK = 8
CAP = 24
EPS = 1e-06
ROPE_BASE = 1000000.0


def shifted_2(x, axis, by):
    length = lax.axis_size(axis)
    return lax.ppermute(x, axis, [(i, (i + by) % length) for i in range(length)])


def rms_scale(values, gain_row):
    mean_sq = jnp.mean(values * values, axis=-1, keepdims=True)
    return values * lax.rsqrt(mean_sq + EPS) * gain_row


def rotate(values, positions):
    half_width = values.shape[-1] // 2
    frequency = ROPE_BASE ** (-jnp.arange(half_width, dtype=jnp.float32) * 2.0 / values.shape[-1])
    angles = positions[:, None] * frequency[None, :]
    cosines = jnp.cos(angles)[:, None, :]
    sine_table = jnp.sin(angles)[:, None, :]
    leading = values[..., :half_width]
    trailing = values[..., half_width:]
    return jnp.concatenate(
        [leading * cosines - trailing * sine_table, trailing * cosines + leading * sine_table],
        axis=-1,
    )


def head_block(q_block, key_rows, value_rows, seg_block, seg_all, pos_block, pos_all, score_scale):
    scores = (
        jnp.einsum("qhd,kd->hqk", q_block, key_rows, preferred_element_type=jnp.float32)
        * score_scale
    )
    allowed = (seg_block[:, None] == seg_all[None, :]) & (pos_all[None, :] <= pos_block[:, None])
    scores = jnp.where(allowed[None], scores, -1e30)
    row_max = jnp.max(scores, axis=-1, keepdims=True)
    shifted = jnp.exp(scores - row_max)
    probability = (shifted / jnp.sum(shifted, axis=-1, keepdims=True)).astype(jnp.bfloat16)
    return jnp.einsum(
        "hqk,kd->qhd", probability, value_rows, preferred_element_type=jnp.float32
    ).astype(jnp.bfloat16)


def expert_rows(grouped, gate_up, down_proj):
    gate_up_out = jnp.einsum("necd,edf->necf", grouped, gate_up, preferred_element_type=jnp.float32)
    half_width = down_proj.shape[1]
    hidden = (jax.nn.silu(gate_up_out[..., :half_width]) * gate_up_out[..., half_width:]).astype(
        jnp.bfloat16
    )
    return jnp.einsum(
        "necf,efd->necd", hidden, down_proj, preferred_element_type=jnp.float32
    ).astype(jnp.bfloat16)


def send_back(results):
    return lax.all_to_all(results, "expert", split_axis=0, concat_axis=0, tiled=True)


def per_device(
    acts,
    norm_gains,
    w_query,
    w_keyval,
    w_out,
    w_gate_up,
    w_down,
    expert_ids,
    gate_weights,
    segment_ids,
):
    device_count = lax.axis_size("expert")
    my_index = lax.axis_index("expert")
    tok_rows = acts.shape[1]
    width = acts.shape[2]
    head_dev = w_query.shape[2] // HD
    local_experts = w_gate_up.shape[1]
    heads_total = head_dev * device_count
    gains = norm_gains[0]
    x_wide = acts[0].astype(jnp.float32)
    normed = rms_scale(x_wide, gains[0]).astype(jnp.bfloat16)
    kv_index = my_index * head_dev // (heads_total // KV)
    query_weight = w_query[0]
    gathered_keyval = lax.all_gather(w_keyval[0], "expert", axis=0, tiled=True)
    head_keyval = lax.dynamic_index_in_dim(gathered_keyval, kv_index, 1, keepdims=False)
    row_piece = lax.all_gather(normed, "expert", axis=0, tiled=True)
    piece_rows = row_piece.shape[0]
    positions = jnp.arange(piece_rows).astype(jnp.float32)
    query_piece_rows = row_piece.shape[0]
    query_positions = jnp.arange(query_piece_rows).astype(jnp.float32)
    queries = jnp.dot(row_piece, query_weight, preferred_element_type=jnp.float32).reshape(
        query_piece_rows, head_dev, HD
    )
    queries = (
        rotate(queries, query_positions)
        .astype(jnp.bfloat16)
        .reshape(query_piece_rows, head_dev * HD)
    )
    keyval = jnp.dot(row_piece, head_keyval, preferred_element_type=jnp.float32)
    key_rows = rotate(keyval[:, None, :HD], positions).astype(jnp.bfloat16).reshape(piece_rows, HD)
    value_rows = keyval[:, HD:].astype(jnp.bfloat16)
    projected = jnp.concatenate([queries, key_rows, value_rows], axis=1)
    tokens = projected.shape[0]
    all_queries = projected[:, : head_dev * HD].reshape(tokens, head_dev, HD)
    all_keys = projected[:, head_dev * HD : (head_dev + 1) * HD]
    all_values = projected[:, (head_dev + 1) * HD :]
    segments = segment_ids[0]
    all_positions = jnp.arange(tokens)
    q_rows = min(512, tokens)
    score_scale = 1.0 / math.sqrt(HD)

    def attend(first_row):
        q_block = lax.dynamic_slice_in_dim(all_queries, first_row, q_rows, 0)
        seg_block = lax.dynamic_slice_in_dim(segments, first_row, q_rows, 0)
        pos_block = first_row + jnp.arange(q_rows)
        return head_block(
            q_block,
            all_keys,
            all_values,
            seg_block,
            segments,
            pos_block,
            all_positions,
            score_scale,
        )

    block_starts = jnp.arange(tokens // q_rows) * q_rows
    attended = lax.map(attend, block_starts).reshape(tokens, head_dev * HD)
    out_weight = w_out[0]
    attention = lax.psum_scatter(
        jnp.dot(attended, out_weight, preferred_element_type=jnp.float32).astype(jnp.bfloat16),
        "expert",
        scatter_dimension=0,
        tiled=True,
    ).astype(jnp.float32)
    middle_wide = (x_wide + attention).astype(jnp.bfloat16).astype(jnp.float32)
    mixer_in = rms_scale(middle_wide, gains[1]).astype(jnp.bfloat16)
    routes_flat = expert_ids[0].reshape(-1)
    onehot = (routes_flat[:, None] == jnp.arange(EXPERTS, dtype=jnp.int32)[None, :]).astype(
        jnp.int32
    )
    earlier = jnp.cumsum(onehot, axis=0) - onehot
    slot_rank = jnp.sum(earlier * onehot, axis=1)
    slot_index = routes_flat * CAP + slot_rank
    routed = jnp.repeat(mixer_in, TOPK, axis=0)
    send_rows = (
        jnp.zeros((EXPERTS * CAP, width), jnp.bfloat16)
        .at[slot_index]
        .set(routed)
        .reshape(EXPERTS, CAP, width)
    )
    gate_up = w_gate_up[0]
    down_proj = w_down[0]
    received = lax.all_to_all(send_rows, "expert", split_axis=0, concat_axis=0, tiled=True)
    source_count = received.shape[0] // local_experts
    grouped = received.reshape(source_count, local_experts, received.shape[1], width)
    outputs = expert_rows(grouped, gate_up, down_proj)
    returned = send_back(outputs.reshape(received.shape))
    picked = (
        returned.reshape(EXPERTS * CAP, width)[slot_index]
        .astype(jnp.float32)
        .reshape(tok_rows, TOPK, width)
    )
    mixed = jnp.sum(picked * gate_weights[0][:, :, None], axis=1)
    result = (middle_wide + mixed).astype(jnp.bfloat16)
    handed = shifted_2(result, "section", 1)
    return handed[None]


def solution(mesh):
    placed = (
        P("section", "expert", None),
        P("section", None, None),
        P("section", None, "expert"),
        P("section", "expert", None, None),
        P("section", "expert", None),
        P("section", "expert", None, None),
        P("section", "expert", None, None),
        P("section", "expert", None),
        P("section", "expert", None),
        P("section", None),
    )
    return jax.shard_map(
        per_device,
        mesh=mesh,
        in_specs=placed,
        out_specs=P("section", "expert", None),
        check_vma=False,
    )
```

profile of v0, /device:TPU:0, one launch (start us, length us, event | category | flops | bytes accessed | tf_op | source)
XLA Modules:
  0.0 406.4 jit_solution(9805289773962117961)
XLA Ops:
  6.5 0.8 fusion.77
  7.4 1.1 fusion.34
  8.5 1.8 fusion.36
  10.3 1.9 copy.12
  12.4 50.0 %all-gather.4.cloned.1.call-done = bf16[512,2048]{1,0:T(8,128)(2,1)} async-done(((bf16[64,2048]{1,0:T(8,128)(2,1)}), bf16[512,2048]{1,0:T(8,128)(2,1)}) %all-gather.4.cloned.1.call-update) | async-done | bytes 2097168 | tf_op jit(solution)/shard_map/all_gather | solution.py:96
  62.4 2.5 convolution_bitcast_fusion
  64.9 71.6 %all-gather.6.cloned.1.call-done = bf16[1,2048,4,256]{3,1,2,0:T(8,128)(2,1)} async-done(((bf16[1,256,4,256]{3,1,2,0:T(8,128)(2,1)}), bf16[1,2048,4,256]{3,1,2,0:T(8,128)(2,1)}) %all-gather.6.cloned.1.call-update) | async-done | bytes 4194320 | tf_op jit(solution)/shard_map/all_gather | solution.py:94
  136.5 2.6 fusion.24
  139.1 0.6 fusion.70
  139.8 0.4 fusion.78
  140.1 0.2 fusion.29
  140.4 2.4 convolution_convert_fusion
  142.8 0.1 eq.59
  143.0 1.2 reduce-window.6
  144.2 0.2 slice_reduce_fusion
  144.6 0.1 mul.210
  144.7 0.1 fusion.68
  144.8 64.6 %reduce-scatter.2.cloned.1.call-done = bf16[64,2048]{1,0:T(8,128)(2,1)} async-done(((bf16[512,2048]{1,0:T(8,128)(2,1)}), bf16[64,2048]{1,0:T(8,128)(2,1)}) %reduce-scatter.2.cloned.1.call-update) | async-done | bytes 262160 | tf_op jit(solution)/shard_map/reduce_scatter | solution.py:140
  209.4 1.1 fusion.30
  210.6 1.8 fusion.32
  212.3 5.0 %scatter_custom_fusion = bf16[768,2048]{1,0:T(8,128)(2,1)S(1)} fusion(s32[512]{0:T(512)S(1)} %bitcast.115, bf16[]{:T(256)} %constant.73.clone.1, bf16[64,2048]{1,0:T(8,128)(2,1)} %fusion.32), kind=kCustom, calls=%fused_computation.15 | custom fusion | bytes 3407874 | tf_op jit(solution)/shard_map/scatter | solution.py:159
  217.3 72.9 %all_to_all.10 = bf16[32,24,2048]{2,1,0:T(8,128)(2,1)S(1)} all-to-all(bf16[32,24,2048]{2,1,0:T(8,128)(2,1)S(1)} %bitcast.110), channel_id=1, replica_groups=mesh['section'=4,'expert'=8] {'expert'}, dimensions={0} | all-to-all | bytes 6291456 | tf_op jit(solution)/shard_map/all_to_all | solution.py:164
  290.3 10.8 %fusion.5 = f32[8,4,24,1536]{3,2,0,1:T(8,128)S(1)} fusion(bf16[1,4,2048,1536]{3,2,1,0:T(8,128)(2,1)} %param.15, bf16[8,4,24,2048]{3,2,1,0:T(8,128)(2,1)S(1)} %bitcast.111), kind=kOutput, calls=%fused_computation.8 | convolution fusion | flops 4831838208 | bytes 33030144 | tf_op jit(solution)/shard_map/necd,edf->necf/dot_general | solution.py:56
  301.1 7.3 %fusion.12 = bf16[8,4,24,2048]{3,2,0,1:T(8,128)(2,1)S(1)} fusion(bf16[1,4,768,2048]{3,2,1,0:T(8,128)(2,1)} %param.16, f32[8,4,24,1536]{3,2,0,1:T(8,128)S(1)} %fusion.5), kind=kOutput, calls=%fused_computation.11 | convolution fusion | flops 2421030912 | bytes 20447232 | tf_op jit(solution)/shard_map/necf,efd->necd/dot_general | solution.py:61
  308.4 1.9 copy.18
  310.3 4.6 %all-to-all-start.1 = ((bf16[32,24,2048]{2,1,0:T(8,128)(2,1)}), bf16[32,24,2048]{2,1,0:T(8,128)(2,1)}, u32[]{:S(2)}, u32[]{:S(2)}) async-start(bf16[32,24,2048]{2,1,0:T(8,128)(2,1)} %bitcast.34), calls=%async_computation.2 | async-start | bytes 6291456 | tf_op jit(solution)/shard_map/all_to_all | solution.py:67
  315.0 69.5 %all-to-all-done.1 = bf16[32,24,2048]{2,1,0:T(8,128)(2,1)} async-done(((bf16[32,24,2048]{2,1,0:T(8,128)(2,1)}), bf16[32,24,2048]{2,1,0:T(8,128)(2,1)}, u32[]{:S(2)}, u32[]{:S(2)}) %all-to-all-start.1) | async-done | bytes 3145760 | tf_op jit(solution)/shard_map/all_to_all | solution.py:67
  384.5 6.8 %gather_fusion = bf16[512,2048]{1,0:T(8,128)(2,1)S(1)} fusion(bf16[768,2048]{1,0:T(8,128)(2,1)} %bitcast.35, s32[1024]{0:T(1024)S(1)} %pad_clamp_fusion), kind=kCustom, calls=%fused_computation | custom fusion | bytes 4196352 | tf_op jit(solution)/shard_map/gather | solution.py:170
  391.3 1.8 fusion.4
  393.2 0.1 fusion.33
  393.3 5.8 %collective-permute-done = bf16[64,2048]{1,0:T(8,128)(2,1)S(1)} collective-permute-done((bf16[64,2048]{1,0:T(8,128)(2,1)S(1)}, bf16[64,2048]{1,0:T(8,128)(2,1)S(1)}, u32[]{:S(2)}, u32[]{:S(2)}) %collective-permute-start) | collective-permute-done | bytes 262176 | tf_op jit(solution)/shard_map/ppermute | solution.py:18
  399.1 0.7 copy.27
  (36 shorter events, 0.7 us)
Async XLA Ops:
  6.5 133.8 %copy-start = (bf16[1,128,2048]{2,1,0:T(8,128)(2,1)S(1)}, bf16[1,128,2048]{2,1,0:T(8,128)(2,1)}, u32[]{:S(2)}) copy-start(bf16[1,128,2048]{2,1,0:T(8,128)(2,1)} %param.14) | copy-start | bytes 1572868
  6.5 55.9 %all-gather.4.cloned.1.call-start = ((), (), s32[]{:S(2)}) async-start(), calls=%async_computation.3 | async-start | bytes 2359296 | tf_op jit(solution)/shard_map/all_gather | solution.py:96
  10.3 126.2 %all-gather.6.cloned.1.call-start = ((), (), s32[]{:S(2)}) async-start(), calls=%async_computation.5 | async-start | bytes 4718592 | tf_op jit(solution)/shard_map/all_gather | solution.py:94
  12.3 197.1 %reduce-scatter.2.cloned.1.call-start = ((), (), s32[]{:S(2)}) async-start(), calls=%async_computation.4 | async-start | bytes 2359296 | tf_op jit(solution)/shard_map/reduce_scatter | solution.py:140
  64.9 74.8 %copy-start.6 = (s32[1,512]{1,0:T(1,128)S(1)}, s32[1,512]{1,0:T(1,128)}, u32[]{:S(2)}) copy-start(s32[1,512]{1,0:T(1,128)} %param.19) | copy-start | bytes 6148
  140.3 2.4 copy-start.4
  140.4 69.0 %copy-start.2 = (bf16[1,64,2048]{2,1,0:T(8,128)(2,1)S(1)}, bf16[1,64,2048]{2,1,0:T(8,128)(2,1)}, u32[]{:S(2)}) copy-start(bf16[1,64,2048]{2,1,0:T(8,128)(2,1)} %param.10) | copy-start | bytes 786436
  310.3 4.6 %copy-start.5 = (f32[1,64,8]{1,2,0:T(8,128)S(1)}, f32[1,64,8]{1,2,0:T(8,128)}, u32[]{:S(2)}) copy-start(f32[1,64,8]{1,2,0:T(8,128)} %param.18) | copy-start | bytes 6148
  310.3 74.2 %all-to-all-start.1 = ((bf16[32,24,2048]{2,1,0:T(8,128)(2,1)}), bf16[32,24,2048]{2,1,0:T(8,128)(2,1)}, u32[]{:S(2)}, u32[]{:S(2)}) async-start(bf16[32,24,2048]{2,1,0:T(8,128)(2,1)} %bitcast.34), calls=%async_computation.2 | async-start | bytes 6291456 | tf_op jit(solution)/shard_map/all_to_all | solution.py:67
  384.5 8.6 %copy-start.3 = (bf16[64,2048]{1,0:T(8,128)(2,1)S(1)}, bf16[64,2048]{1,0:T(8,128)(2,1)}, u32[]{:S(2)}) copy-start(bf16[64,2048]{1,0:T(8,128)(2,1)} %reduce-scatter.2.cloned.1.call-done) | copy-start | bytes 786436
  384.5 15.3 %copy-start.1 = (bf16[1,128,2048]{2,1,0:T(8,128)(2,1)S(1)}, bf16[1,128,2048]{2,1,0:T(8,128)(2,1)}, u32[]{:S(2)}) copy-start(bf16[1,128,2048]{2,1,0:T(8,128)(2,1)} %param.14) | copy-start | bytes 1572868
  393.3 5.8 %collective-permute-start = (bf16[64,2048]{1,0:T(8,128)(2,1)S(1)}, bf16[64,2048]{1,0:T(8,128)(2,1)S(1)}, u32[]{:S(2)}, u32[]{:S(2)}) collective-permute-start(bf16[64,2048]{1,0:T(8,128)(2,1)S(1)} %fusion.33), channel_id=1, source_target_pairs={{0,8},{8,16},{16,24},{24,0},{1,9},{9,17},{17,25},{25,1},{2,10},{10... | collective-permute-start | bytes 786440 | tf_op jit(solution)/shard_map/ppermute | solution.py:18
Sparse Core Ops, SparseCore 0:
  10.4 51.9 all-gather.3
  64.6 71.8 all-gather.5
  142.9 66.4 reduce-scatter.1
where the time goes:
time: 407 us; the launch traced here: 406 us
  waiting for transfers between devices  262 us (64%)
  blocking collectives  72.9 us (18%)
  matrix products  25.9 us (6%)
  local copies, waits for them, and re-layouts  18 us (4%)
  between operations  13.3 us (3%)
  other arithmetic  9.89 us (2%)
  starting transfers between devices  4.71 us (1%)
    all_to_all x1, blocking collectives, per_device(): lax.all_to_all(send_rows, 'expert', split_axis=0, concat_axis=0, tiled=True)  72.9 us
    all_gather x1, waiting for transfers between devices, per_device(): gathered_keyval = lax.all_gather(w_keyval[0], 'expert', axis=0, tiled=True)  71.6 us
    all_to_all x1, waiting for transfers between devices, send_back(): lax.all_to_all(results, 'expert', split_axis=0, concat_axis=0, tiled=True)  69.5 us
    reduce_scatter x1, waiting for transfers between devices, per_device(): lax.psum_scatter(jnp.dot(attended, out_weight, preferred_element_type=jnp...  64.6 us
    all_gather x1, waiting for transfers between devices, per_device(): row_piece = lax.all_gather(normed, 'expert', axis=0, tiled=True)  50 us
    dot_general x1, matrix products, expert_rows(): jnp.einsum('necd,edf->necf', grouped, gate_up, preferred_element_type=jnp...  10.8 us
  transfers between devices with their start and end apart: 5, of which 5 were waited for; matrix products, arithmetic and copies ran while one was open for 2% of the time, Pallas kernels for 0%

commit v1 on v0

--- a/solution.py
+++ b/solution.py
@@ -11,6 +11,17 @@
 CAP = 24
 EPS = 1e-06
 ROPE_BASE = 1000000.0
+
+
+def around_the_ring(x, mesh_axis, d):
+    size = lax.axis_size(mesh_axis)
+    right = [(i, (i + 1) % size) for i in range(size)]
+    parts = [x]
+    for stride in range(1, size):
+        parts = [lax.ppermute(parts[0], mesh_axis, right), *parts]
+    whole = jnp.concatenate(parts, axis=d)
+    shift = (lax.axis_index(mesh_axis) + 1) * parts[-1].shape[d]
+    return jnp.roll(whole, shift, axis=d)
 
 
 def shifted_2(x, axis, by):
@@ -91,7 +102,7 @@
     normed = rms_scale(x_wide, gains[0]).astype(jnp.bfloat16)
     kv_index = my_index * head_dev // (heads_total // KV)
     query_weight = w_query[0]
-    gathered_keyval = lax.all_gather(w_keyval[0], "expert", axis=0, tiled=True)
+    gathered_keyval = around_the_ring(w_keyval[0], "expert", 0)
     head_keyval = lax.dynamic_index_in_dim(gathered_keyval, kv_index, 1, keepdims=False)
     row_piece = lax.all_gather(normed, "expert", axis=0, tiled=True)
     piece_rows = row_piece.shape[0]

time: 407 us -> 410 us (level)
  waiting for transfers between devices: 262 us -> 243 us
  local copies, waits for them, and re-layouts: 18 us -> 36.7 us
    ppermute x0 -> x7, waiting for transfers between devices: none -> 102 us  [around_the_ring(): parts = [lax.ppermute(parts[0], mesh_axis, right), *parts]]
    all_gather x1 -> x0, waiting for transfers between devices: 71.6 us -> none  [per_device(): gathered_keyval = lax.all_gather(w_keyval[0], 'expert', axis=0, tiled=True)]
    all_gather x1, waiting for transfers between devices: 50 us -> 0.01 us  [per_device(): row_piece = lax.all_gather(normed, 'expert', axis=0, tiled=True)]
    unnamed x17 -> x34, local copies, waits for them, and re-layouts: 2.74 us -> 20.6 us
  transfers between devices with their start and end apart: 5 -> 11, of which waited for: 5 -> 10; matrix products, arithmetic and copies ran while one was open for 2% -> 6% of each run, Pallas kernels for 0% -> 0%
where the time goes in v1:
time: 410 us; the launch traced here: 409 us
  waiting for transfers between devices  243 us (59%)
  blocking collectives  72.9 us (18%)
  local copies, waits for them, and re-layouts  36.7 us (9%)
  matrix products  26 us (6%)
  between operations  13.6 us (3%)
  other arithmetic  9.88 us (2%)
  starting transfers between devices  7.54 us (2%)
    ppermute x7, waiting for transfers between devices, around_the_ring(): parts = [lax.ppermute(parts[0], mesh_axis, right), *parts]  102 us
    all_to_all x1, blocking collectives, per_device(): lax.all_to_all(send_rows, 'expert', split_axis=0, concat_axis=0, tiled=True)  72.9 us
    all_to_all x1, waiting for transfers between devices, send_back(): lax.all_to_all(results, 'expert', split_axis=0, concat_axis=0, tiled=True)  69.5 us
    reduce_scatter x1, waiting for transfers between devices, per_device(): lax.psum_scatter(jnp.dot(attended, out_weight, preferred_element_type=jnp...  65 us
    unnamed x34, local copies, waits for them, and re-layouts  20.6 us
    dot_general x1, matrix products, expert_rows(): jnp.einsum('necd,edf->necf', grouped, gate_up, preferred_element_type=jnp...  10.8 us
  transfers between devices with their start and end apart: 11, of which 10 were waited for; matrix products, arithmetic and copies ran while one was open for 6% of the time, Pallas kernels for 0%

profile of v1, /device:TPU:0, one launch (start us, length us, event | category | flops | bytes accessed | tf_op | source)
XLA Modules:
  0.0 409.4 jit_solution(3040787108882928086)
XLA Ops:
  6.5 1.2 copy.31
  7.7 3.0 collective-permute-start
  10.7 15.0 %collective-permute-done = bf16[256,4,256]{2,0,1:T(8,128)(2,1)S(1)} collective-permute-done((bf16[256,4,256]{2,0,1:T(8,128)(2,1)S(1)}, bf16[256,4,256]{2,0,1:T(8,128)(2,1)S(1)}, u32[]{:S(2)}, u32[]{:S(2)}) %collective-permute-start) | collective-permute-done | bytes 524320 | tf_op jit(solution)/shard_map/ppermute | solution.py:21
  25.7 15.8 %collective-permute-done.1 = bf16[256,4,256]{2,0,1:T(8,128)(2,1)S(1)} collective-permute-done((bf16[256,4,256]{2,0,1:T(8,128)(2,1)S(1)}, bf16[256,4,256]{2,0,1:T(8,128)(2,1)S(1)}, u32[]{:S(2)}, u32[]{:S(2)}) %collective-permute-start.1) | collective-permute-done | bytes 524320 | tf_op jit(solution)/shard_map/ppermute | solution.py:21
  42.6 13.8 %collective-permute-done.2 = bf16[256,4,256]{2,0,1:T(8,128)(2,1)S(1)} collective-permute-done((bf16[256,4,256]{2,0,1:T(8,128)(2,1)S(1)}, bf16[256,4,256]{2,0,1:T(8,128)(2,1)S(1)}, u32[]{:S(2)}, u32[]{:S(2)}) %collective-permute-start.2) | collective-permute-done | bytes 524320 | tf_op jit(solution)/shard_map/ppermute | solution.py:21
  57.2 13.1 %collective-permute-done.3 = bf16[256,4,256]{2,0,1:T(8,128)(2,1)S(1)} collective-permute-done((bf16[256,4,256]{2,0,1:T(8,128)(2,1)S(1)}, bf16[256,4,256]{2,0,1:T(8,128)(2,1)S(1)}, u32[]{:S(2)}, u32[]{:S(2)}) %collective-permute-start.3) | collective-permute-done | bytes 524320 | tf_op jit(solution)/shard_map/ppermute | solution.py:21
  70.4 1.8 fusion.36
  72.2 11.3 %collective-permute-done.4 = bf16[256,4,256]{2,0,1:T(8,128)(2,1)} collective-permute-done((bf16[256,4,256]{2,0,1:T(8,128)(2,1)S(1)}, bf16[256,4,256]{2,0,1:T(8,128)(2,1)}, u32[]{:S(2)}, u32[]{:S(2)}) %collective-permute-start.4) | collective-permute-done | bytes 524320 | tf_op jit(solution)/shard_map/ppermute | solution.py:21
  83.5 20.9 %collective-permute-done.5 = bf16[256,4,256]{2,0,1:T(8,128)(2,1)} collective-permute-done((bf16[256,4,256]{2,0,1:T(8,128)(2,1)}, bf16[256,4,256]{2,0,1:T(8,128)(2,1)}, u32[]{:S(2)}, u32[]{:S(2)}) %collective-permute-start.5) | collective-permute-done | bytes 524320 | tf_op jit(solution)/shard_map/ppermute | solution.py:21
  104.4 12.5 %collective-permute-done.6 = bf16[256,4,256]{2,0,1:T(8,128)(2,1)} collective-permute-done((bf16[256,4,256]{2,0,1:T(8,128)(2,1)}, bf16[256,4,256]{2,0,1:T(8,128)(2,1)}, u32[]{:S(2)}, u32[]{:S(2)}) %collective-permute-start.6) | collective-permute-done | bytes 524320 | tf_op jit(solution)/shard_map/ppermute | solution.py:21
  116.9 1.8 constant_dynamic-update-slice_fusion.15
  118.8 1.9 constant_dynamic-update-slice_fusion.14
  120.6 1.9 constant_dynamic-update-slice_fusion.13
  126.6 1.9 constant_dynamic-update-slice_fusion.7
  128.5 1.9 constant_dynamic-update-slice_fusion.6
  130.4 1.9 constant_dynamic-update-slice_fusion.5
  136.4 2.6 fusion.24
  139.1 2.5 convolution_bitcast_fusion
  142.8 2.4 convolution_convert_fusion
  145.5 1.2 reduce-window.6
  147.2 65.0 %reduce-scatter.2.cloned.1.call-done = bf16[64,2048]{1,0:T(8,128)(2,1)} async-done(((bf16[512,2048]{1,0:T(8,128)(2,1)}), bf16[64,2048]{1,0:T(8,128)(2,1)}) %reduce-scatter.2.cloned.1.call-update) | async-done | bytes 262160 | tf_op jit(solution)/shard_map/reduce_scatter | solution.py:151
  213.4 1.8 fusion.32
  215.2 5.0 %scatter_custom_fusion = bf16[768,2048]{1,0:T(8,128)(2,1)S(1)} fusion(s32[512]{0:T(512)S(1)} %bitcast.123, bf16[]{:T(256)} %constant.113.clone.1, bf16[64,2048]{1,0:T(8,128)(2,1)} %fusion.32), kind=kCustom, calls=%fused_computation.15 | custom fusion | bytes 3407874 | tf_op jit(solution)/shard_map/scatter | solution.py:170
  220.2 72.9 %all_to_all.10 = bf16[32,24,2048]{2,1,0:T(8,128)(2,1)S(1)} all-to-all(bf16[32,24,2048]{2,1,0:T(8,128)(2,1)S(1)} %bitcast.117), channel_id=1, replica_groups=mesh['section'=4,'expert'=8] {'expert'}, dimensions={0} | all-to-all | bytes 6291456 | tf_op jit(solution)/shard_map/all_to_all | solution.py:175
  293.1 10.8 %fusion.5 = f32[8,4,24,1536]{3,2,0,1:T(8,128)S(1)} fusion(bf16[1,4,2048,1536]{3,2,1,0:T(8,128)(2,1)} %param.15, bf16[8,4,24,2048]{3,2,1,0:T(8,128)(2,1)S(1)} %bitcast.118), kind=kOutput, calls=%fused_computation.8 | convolution fusion | flops 4831838208 | bytes 33030144 | tf_op jit(solution)/shard_map/necd,edf->necf/dot_general | solution.py:67
  303.9 7.3 %fusion.12 = bf16[8,4,24,2048]{3,2,0,1:T(8,128)(2,1)S(1)} fusion(bf16[1,4,768,2048]{3,2,1,0:T(8,128)(2,1)} %param.16, f32[8,4,24,1536]{3,2,0,1:T(8,128)S(1)} %fusion.5), kind=kOutput, calls=%fused_computation.11 | convolution fusion | flops 2421030912 | bytes 20447232 | tf_op jit(solution)/shard_map/necf,efd->necd/dot_general | solution.py:72
  311.3 1.9 copy.18
  313.2 4.4 %all-to-all-start.1 = ((bf16[32,24,2048]{2,1,0:T(8,128)(2,1)}), bf16[32,24,2048]{2,1,0:T(8,128)(2,1)}, u32[]{:S(2)}, u32[]{:S(2)}) async-start(bf16[32,24,2048]{2,1,0:T(8,128)(2,1)} %bitcast.35), calls=%async_computation.2 | async-start | bytes 6291456 | tf_op jit(solution)/shard_map/all_to_all | solution.py:78
  317.7 69.5 %all-to-all-done.1 = bf16[32,24,2048]{2,1,0:T(8,128)(2,1)} async-done(((bf16[32,24,2048]{2,1,0:T(8,128)(2,1)}), bf16[32,24,2048]{2,1,0:T(8,128)(2,1)}, u32[]{:S(2)}, u32[]{:S(2)}) %all-to-all-start.1) | async-done | bytes 3145760 | tf_op jit(solution)/shard_map/all_to_all | solution.py:78
  387.3 6.8 %gather_fusion = bf16[512,2048]{1,0:T(8,128)(2,1)S(1)} fusion(bf16[768,2048]{1,0:T(8,128)(2,1)} %bitcast.36, s32[1024]{0:T(1024)S(1)} %pad_clamp_fusion), kind=kCustom, calls=%fused_computation | custom fusion | bytes 4196352 | tf_op jit(solution)/shard_map/gather | solution.py:181
  394.0 1.8 fusion.4
  396.1 5.8 %collective-permute-done.7 = bf16[64,2048]{1,0:T(8,128)(2,1)S(1)} collective-permute-done((bf16[64,2048]{1,0:T(8,128)(2,1)S(1)}, bf16[64,2048]{1,0:T(8,128)(2,1)S(1)}, u32[]{:S(2)}, u32[]{:S(2)}) %collective-permute-start.7) | collective-permute-done | bytes 262176 | tf_op jit(solution)/shard_map/ppermute | solution.py:29
  (65 shorter events, 14.4 us)
Async XLA Ops:
  6.5 136.3 %copy-start = (bf16[1,128,2048]{2,1,0:T(8,128)(2,1)S(1)}, bf16[1,128,2048]{2,1,0:T(8,128)(2,1)}, u32[]{:S(2)}) copy-start(bf16[1,128,2048]{2,1,0:T(8,128)(2,1)} %param.14) | copy-start | bytes 1572868
  6.5 119.2 %copy-start.3 = (bf16[1,256,4,256]{3,2,1,0:T(4,128)(2,1)S(1)}, bf16[1,256,4,256]{3,2,1,0:T(4,128)(2,1)}, u32[]{:S(2)}) copy-start(bf16[1,256,4,256]{3,2,1,0:T(4,128)(2,1)} %param.13) | copy-start | bytes 1572868
  6.5 129.8 %all-gather.2.cloned.1.call-start = ((), (), s32[]{:S(2)}) async-start(), calls=%async_computation.3 | async-start | bytes 2359296 | tf_op jit(solution)/shard_map/all_gather | solution.py:107
  7.7 18.0 %collective-permute-start = (bf16[256,4,256]{2,0,1:T(8,128)(2,1)S(1)}, bf16[256,4,256]{2,0,1:T(8,128)(2,1)S(1)}, u32[]{:S(2)}, u32[]{:S(2)}) collective-permute-start(bf16[256,4,256]{2,0,1:T(8,128)(2,1)S(1)} %bitcast.119), channel_id=1, source_target_pairs={{0,1},{1,2},{2,3},{3,4},{4,5},{5,6},{6,7},{7,0},{8,9},{9,10},{10,1... | collective-permute-start | bytes 1572872 | tf_op jit(solution)/shard_map/ppermute | solution.py:21
  25.7 15.8 %collective-permute-start.1 = (bf16[256,4,256]{2,0,1:T(8,128)(2,1)S(1)}, bf16[256,4,256]{2,0,1:T(8,128)(2,1)S(1)}, u32[]{:S(2)}, u32[]{:S(2)}) collective-permute-start(bf16[256,4,256]{2,0,1:T(8,128)(2,1)S(1)} %collective-permute-done), channel_id=1, source_target_pairs={{0,1},{1,2},{2,3},{3,4},{4,5},{5,6},{6,7},{7,0},{8,9},{9,10},{10,1... | collective-permute-start | bytes 1572872 | tf_op jit(solution)/shard_map/ppermute | solution.py:21
  41.5 14.9 %collective-permute-start.2 = (bf16[256,4,256]{2,0,1:T(8,128)(2,1)S(1)}, bf16[256,4,256]{2,0,1:T(8,128)(2,1)S(1)}, u32[]{:S(2)}, u32[]{:S(2)}) collective-permute-start(bf16[256,4,256]{2,0,1:T(8,128)(2,1)S(1)} %collective-permute-done.1), channel_id=1, source_target_pairs={{0,1},{1,2},{2,3},{3,4},{4,5},{5,6},{6,7},{7,0},{8,9},{9,10},{10,1... | collective-permute-start | bytes 1572872 | tf_op jit(solution)/shard_map/ppermute | solution.py:21
  56.4 14.0 %collective-permute-start.3 = (bf16[256,4,256]{2,0,1:T(8,128)(2,1)S(1)}, bf16[256,4,256]{2,0,1:T(8,128)(2,1)S(1)}, u32[]{:S(2)}, u32[]{:S(2)}) collective-permute-start(bf16[256,4,256]{2,0,1:T(8,128)(2,1)S(1)} %collective-permute-done.2), channel_id=1, source_target_pairs={{0,1},{1,2},{2,3},{3,4},{4,5},{5,6},{6,7},{7,0},{8,9},{9,10},{10,1... | collective-permute-start | bytes 1572872 | tf_op jit(solution)/shard_map/ppermute | solution.py:21
  70.4 13.1 %collective-permute-start.4 = (bf16[256,4,256]{2,0,1:T(8,128)(2,1)S(1)}, bf16[256,4,256]{2,0,1:T(8,128)(2,1)}, u32[]{:S(2)}, u32[]{:S(2)}) collective-permute-start(bf16[256,4,256]{2,0,1:T(8,128)(2,1)S(1)} %collective-permute-done.3), channel_id=1, source_target_pairs={{0,1},{1,2},{2,3},{3,4},{4,5},{5,6},{6,7},{7,0},{8,9},{9,10},{10,1... | collective-permute-start | bytes 1572872 | tf_op jit(solution)/shard_map/ppermute | solution.py:21
  72.2 140.1 %reduce-scatter.2.cloned.1.call-start = ((), (), s32[]{:S(2)}) async-start(), calls=%async_computation.4 | async-start | bytes 2359296 | tf_op jit(solution)/shard_map/reduce_scatter | solution.py:151
  83.5 20.9 %collective-permute-start.5 = (bf16[256,4,256]{2,0,1:T(8,128)(2,1)}, bf16[256,4,256]{2,0,1:T(8,128)(2,1)}, u32[]{:S(2)}, u32[]{:S(2)}) collective-permute-start(bf16[256,4,256]{2,0,1:T(8,128)(2,1)} %collective-permute-done.4), channel_id=1, source_target_pairs={{0,1},{1,2},{2,3},{3,4},{4,5},{5,6},{6,7},{7,0},{8,9},{9,10},{10,1... | collective-permute-start | bytes 1572872 | tf_op jit(solution)/shard_map/ppermute | solution.py:21
  104.4 12.6 %collective-permute-start.6 = (bf16[256,4,256]{2,0,1:T(8,128)(2,1)}, bf16[256,4,256]{2,0,1:T(8,128)(2,1)}, u32[]{:S(2)}, u32[]{:S(2)}) collective-permute-start(bf16[256,4,256]{2,0,1:T(8,128)(2,1)} %collective-permute-done.5), channel_id=1, source_target_pairs={{0,1},{1,2},{2,3},{3,4},{4,5},{5,6},{6,7},{7,0},{8,9},{9,10},{10,1... | collective-permute-start | bytes 1572872 | tf_op jit(solution)/shard_map/ppermute | solution.py:21
  128.5 13.7 %copy-start.7 = (s32[1,512]{1,0:T(1,128)S(1)}, s32[1,512]{1,0:T(1,128)}, u32[]{:S(2)}) copy-start(s32[1,512]{1,0:T(1,128)} %param.19) | copy-start | bytes 6148
  139.0 6.2 %copy-start.5 = (s32[1,64,8]{1,2,0:T(8,128)S(1)}, s32[1,64,8]{1,2,0:T(8,128)}, u32[]{:S(2)}) copy-start(s32[1,64,8]{1,2,0:T(8,128)} %param.17) | copy-start | bytes 6148
  139.0 73.2 %copy-start.2 = (bf16[1,64,2048]{2,1,0:T(8,128)(2,1)S(1)}, bf16[1,64,2048]{2,1,0:T(8,128)(2,1)}, u32[]{:S(2)}) copy-start(bf16[1,64,2048]{2,1,0:T(8,128)(2,1)} %param.10) | copy-start | bytes 786436
  311.2 6.4 %copy-start.6 = (f32[1,64,8]{1,2,0:T(8,128)S(1)}, f32[1,64,8]{1,2,0:T(8,128)}, u32[]{:S(2)}) copy-start(f32[1,64,8]{1,2,0:T(8,128)} %param.18) | copy-start | bytes 6148
  313.2 74.1 %all-to-all-start.1 = ((bf16[32,24,2048]{2,1,0:T(8,128)(2,1)}), bf16[32,24,2048]{2,1,0:T(8,128)(2,1)}, u32[]{:S(2)}, u32[]{:S(2)}) async-start(bf16[32,24,2048]{2,1,0:T(8,128)(2,1)} %bitcast.35), calls=%async_computation.2 | async-start | bytes 6291456 | tf_op jit(solution)/shard_map/all_to_all | solution.py:78
  387.3 15.3 %copy-start.1 = (bf16[1,128,2048]{2,1,0:T(8,128)(2,1)S(1)}, bf16[1,128,2048]{2,1,0:T(8,128)(2,1)}, u32[]{:S(2)}) copy-start(bf16[1,128,2048]{2,1,0:T(8,128)(2,1)} %param.14) | copy-start | bytes 1572868
  387.3 8.6 %copy-start.4 = (bf16[64,2048]{1,0:T(8,128)(2,1)S(1)}, bf16[64,2048]{1,0:T(8,128)(2,1)}, u32[]{:S(2)}) copy-start(bf16[64,2048]{1,0:T(8,128)(2,1)} %reduce-scatter.2.cloned.1.call-done) | copy-start | bytes 786436
  396.0 5.8 %collective-permute-start.7 = (bf16[64,2048]{1,0:T(8,128)(2,1)S(1)}, bf16[64,2048]{1,0:T(8,128)(2,1)S(1)}, u32[]{:S(2)}, u32[]{:S(2)}) collective-permute-start(bf16[64,2048]{1,0:T(8,128)(2,1)S(1)} %fusion.33), channel_id=1, source_target_pairs={{0,8},{8,16},{16,24},{24,0},{1,9},{9,17},{17,25},{25,1},{2,10},{10... | collective-permute-start | bytes 786440 | tf_op jit(solution)/shard_map/ppermute | solution.py:29
Sparse Core Ops, SparseCore 0:
  72.3 62.1 all-gather.1
  145.3 66.9 reduce-scatter.1
